TPU v7x, 32 devices: a whole 2x2x4 slice. The times are simulated.
32 devices in a mesh: dp: 4 (over y, x), seq: 2 (over core), tensor: 4 (over z).
Axes of the slice: x: 2, y: 2, z: 4, core: 2. Of those that a mesh axis runs over, the one named last changes fastest.
Arguments:
- block_input: float32 [4, 16, 256, 1024], P('dp', 'seq', 'tensor'), may hold values from -6 to 6
- w_qkv: bfloat16 [1024, 3, 1024], P(None, None, 'tensor'), may hold values from -0.1875 to 0.1875
- qv_bias: bfloat16 [2, 1024], P(None, 'tensor'), may hold values from -3 to 3
- w_out: bfloat16 [1024, 1024], P('tensor'), may hold values from -3 to 3
- b_out: bfloat16 [1024], replicated, may hold values from -3 to 3
- w_up: bfloat16 [1024, 4096], P(None, 'tensor'), may hold values from -0.1875 to 0.1875
- b_up: bfloat16 [4096], P('tensor'), may hold values from -3 to 3
- w_down: bfloat16 [4096, 1024], P('tensor'), may hold values from -0.09375 to 0.09375
- b_down: bfloat16 [1024], replicated, may hold values from -3 to 3
- w_mod: bfloat16 [1024, 6144], replicated, may hold values from -0.375 to 0.375
- b_mod: bfloat16 [6144], replicated, may hold values from -3 to 3
- context_frames: int32 [4], P('dp'), may hold values from 1 to 15
- noise_levels: int32 [4, 16], P('dp', 'seq'), may hold values from 0 to 999
- cotangent: float32 [4, 16, 256, 1024], P('dp', 'seq', 'tensor'), may hold values from -6 to 6
Outputs:
- output: float32 [4, 16, 256, 1024], P('dp', 'seq', 'tensor')
- grad_input: float32 [4, 16, 256, 1024], P('dp', 'seq', 'tensor')
- grad_w_qkv: float32 [1024, 3, 1024], P(None, None, 'tensor')
- grad_qv_bias: float32 [2, 1024], P(None, 'tensor')
- grad_w_out: float32 [1024, 1024], P('tensor')
- grad_b_out: float32 [1024], P('tensor')
- grad_w_up: float32 [1024, 4096], P(None, 'tensor')
- grad_b_up: float32 [4096], P('tensor')
- grad_w_down: float32 [4096, 1024], P('tensor')
- grad_b_down: float32 [1024], P('tensor')
- grad_w_mod: float32 [1024, 6144], P(None, 'tensor')
- grad_b_mod: float32 [6144], P('tensor')
Inputs may be any that keep to these rules, and one draw needn't show every extreme that they name: `noise_levels`: noise level index of each frame.
All inputs are finite; a program needn't handle non-finite values.
Results may differ from a plain program's by a relative error of at most 0.02.
Values may be sent and summed in bfloat16 or wider, within the bound.
No kernel may reach another device: no remote copies, remote signals or barrier semaphores. Data moves between devices by JAX's collectives and lax.ppermute only.
A program may use at most 256 MiB of HBM per device.

v0:
```python
import math
import jax
import jax.numpy as jnp
from jax import lax
from jax.sharding import PartitionSpec as P

HD = 64


def level_features(levels, context, frame_ids, breadth):
    level_used = jnp.where(frame_ids[None, :] < context[:, None], 0, levels).astype(jnp.float32)
    halfway = breadth // 2
    frequency = jnp.exp(-math.log(10000.0) * jnp.arange(halfway, dtype=jnp.float32) / halfway)
    angles = level_used[..., None] * frequency
    return jax.nn.silu(jnp.concatenate([jnp.cos(angles), jnp.sin(angles)], axis=-1))


def normalize(stream):
    centre = stream - jnp.mean(stream, axis=-1, keepdims=True)
    inverse = lax.rsqrt(jnp.mean(centre * centre, axis=-1, keepdims=True) + 1e-06)
    return (centre * inverse, inverse)


def norm_back(grad_normed, normed, inverse):
    first_mean = jnp.mean(grad_normed, axis=-1, keepdims=True)
    second_mean = jnp.mean(grad_normed * normed, axis=-1, keepdims=True)
    return inverse * (grad_normed - first_mean - normed * second_mean)


def gelu_back(pre_act, grad_act):
    _, pullback = jax.vjp(lambda argument: jax.nn.gelu(argument, approximate=True), pre_act)
    return pullback(grad_act)[0]


def body(
    block_input,
    w_qkv,
    qv_bias,
    w_out,
    b_out,
    w_up,
    b_up,
    w_down,
    b_down,
    w_mod,
    b_mod,
    context_frames,
    noise_levels,
    cotangent,
):
    clip_count, half_frames, patch_local, breadth = block_input.shape
    patches_all = patch_local * lax.axis_size("tensor")
    head_cols = w_qkv.shape[2]
    heads_local = head_cols // HD
    softmax_scale = HD ** (-0.5)
    frame_first = lax.axis_index("seq") * half_frames
    frame_ids = frame_first + jnp.arange(half_frames, dtype=jnp.int32)
    condition = level_features(noise_levels, context_frames, frame_ids, breadth).astype(
        jnp.bfloat16
    )
    modulation = jnp.einsum(
        "cfd,de->cfe", condition, w_mod, preferred_element_type=jnp.float32
    ) + b_mod.astype(jnp.float32)
    shift_one, scale_one, gate_one, shift_two, scale_two, gate_two = jnp.split(
        modulation[:, :, None, :], 6, axis=-1
    )
    normed_one, inverse_one = normalize(block_input)
    attn_in = (normed_one * (1.0 + scale_one) + shift_one).astype(jnp.bfloat16)
    attn_all = lax.all_gather(attn_in, "tensor", axis=2, tiled=True)
    projected = jnp.einsum("cfpd,dke->cfpke", attn_all, w_qkv, preferred_element_type=jnp.float32)
    bias_float = qv_bias.astype(jnp.float32)
    queries = (projected[..., 0, :] + bias_float[0]).astype(jnp.bfloat16)
    key_local = projected[..., 1, :].astype(jnp.bfloat16)
    value_local = (projected[..., 2, :] + bias_float[1]).astype(jnp.bfloat16)
    key_clip, value_clip = (
        lax.all_gather(key_local, "seq", axis=1, tiled=True),
        lax.all_gather(value_local, "seq", axis=1, tiled=True),
    )
    query_rows = half_frames * patches_all
    block_rows = min(512, query_rows)
    block_count = query_rows // block_rows
    key_rows = key_clip.shape[1] * patches_all
    key_frame = jnp.arange(key_rows, dtype=jnp.int32) // patches_all
    query_frames = (frame_first + jnp.arange(query_rows, dtype=jnp.int32) // patches_all).reshape(
        block_count, block_rows
    )
    query_heads = queries.reshape(clip_count, block_count, block_rows, heads_local, HD)
    key_heads = key_clip.reshape(clip_count, key_rows, heads_local, HD)
    value_heads = value_clip.reshape(clip_count, key_rows, heads_local, HD)

    def masked_scores(query_block, keys, frames_block, context_limit):
        scores = (
            jnp.einsum("bhd,khd->hbk", query_block, keys, preferred_element_type=jnp.float32)
            * softmax_scale
        )
        allowed = (key_frame[None, :] <= frames_block[:, None]) | (
            key_frame[None, :] < context_limit
        )
        return jnp.where(allowed[None], scores, -1e30)

    def forward_clip(members):
        clip_queries, keys, values, context_limit = members

        def forward_block(slices):
            query_block, frames_block = slices
            scores = masked_scores(query_block, keys, frames_block, context_limit)
            row_max = jnp.max(scores, axis=-1, keepdims=True)
            exponent = jnp.exp(scores - row_max)
            denominator = jnp.sum(exponent, axis=-1, keepdims=True)
            probability = (exponent / denominator).astype(jnp.bfloat16)
            result = jnp.einsum(
                "hbk,khd->bhd", probability, values, preferred_element_type=jnp.float32
            )
            return (result.astype(jnp.bfloat16), (row_max + jnp.log(denominator))[..., 0])

        return lax.map(forward_block, (clip_queries, query_frames))

    attended, log_total = lax.map(
        forward_clip, (query_heads, key_heads, value_heads, context_frames)
    )
    attended_rows = attended.reshape(clip_count, half_frames, patches_all, head_cols)
    portion = attended_rows
    branch_rows = lax.psum_scatter(
        jnp.einsum("cfpe,ed->pcfd", portion, w_out, preferred_element_type=jnp.float32).astype(
            jnp.bfloat16
        ),
        "tensor",
        scatter_dimension=0,
        tiled=True,
    ).astype(jnp.float32)
    branch_one = jnp.transpose(branch_rows, (1, 2, 0, 3)) + b_out.astype(jnp.float32)
    hidden_one = block_input + gate_one * branch_one
    normed_two, inverse_two = normalize(hidden_one)
    mlp_in = (normed_two * (1.0 + scale_two) + shift_two).astype(jnp.bfloat16)
    mlp_all = lax.all_gather(mlp_in, "tensor", axis=2, tiled=True)
    pre_act = jnp.einsum(
        "cfpd,de->cfpe", mlp_all, w_up, preferred_element_type=jnp.float32
    ) + b_up.astype(jnp.float32)
    activated = jax.nn.gelu(pre_act, approximate=True).astype(jnp.bfloat16)
    portion = activated
    mlp_rows = lax.psum_scatter(
        jnp.einsum("cfpe,ed->pcfd", portion, w_down, preferred_element_type=jnp.float32).astype(
            jnp.bfloat16
        ),
        "tensor",
        scatter_dimension=0,
        tiled=True,
    ).astype(jnp.float32)
    mlp_out = jnp.transpose(mlp_rows, (1, 2, 0, 3)) + b_down.astype(jnp.float32)
    output = hidden_one + gate_two * mlp_out
    grad_mlp = gate_two * cotangent
    grad_gate_two = jnp.sum(cotangent * mlp_out, axis=2)
    grad_b_down = jnp.sum(grad_mlp, axis=(0, 1, 2))
    grad_mlp_low = grad_mlp.astype(jnp.bfloat16)
    grad_mlp_all = lax.all_gather(grad_mlp_low, "tensor", axis=2, tiled=True)
    grad_act = jnp.einsum("cfpd,ed->cfpe", grad_mlp_all, w_down, preferred_element_type=jnp.float32)
    grad_w_down = jnp.einsum(
        "cfpe,cfpd->ed", activated, grad_mlp_all, preferred_element_type=jnp.float32
    )
    grad_pre = gelu_back(pre_act, grad_act).astype(jnp.bfloat16)
    grad_b_up = jnp.sum(grad_pre.astype(jnp.float32), axis=(0, 1, 2))
    grad_w_up = jnp.einsum("cfpd,cfpe->de", mlp_all, grad_pre, preferred_element_type=jnp.float32)
    portion = grad_pre
    grad_mlp_rows = lax.psum_scatter(
        jnp.einsum("cfpe,de->pcfd", portion, w_up, preferred_element_type=jnp.float32).astype(
            jnp.bfloat16
        ),
        "tensor",
        scatter_dimension=0,
        tiled=True,
    ).astype(jnp.float32)
    grad_mlp_in = jnp.transpose(grad_mlp_rows, (1, 2, 0, 3))
    grad_shift_two = jnp.sum(grad_mlp_in, axis=2)
    grad_scale_two = jnp.sum(grad_mlp_in * normed_two, axis=2)
    grad_hidden = cotangent + norm_back(grad_mlp_in * (1.0 + scale_two), normed_two, inverse_two)
    grad_branch = gate_one * grad_hidden
    grad_gate_one = jnp.sum(grad_hidden * branch_one, axis=2)
    grad_b_out = jnp.sum(grad_branch, axis=(0, 1, 2))
    grad_branch_all = lax.all_gather(grad_branch.astype(jnp.bfloat16), "tensor", axis=2, tiled=True)
    grad_attended = jnp.einsum(
        "cfpd,ed->cfpe", grad_branch_all, w_out, preferred_element_type=jnp.float32
    ).astype(jnp.bfloat16)
    grad_w_out = jnp.einsum(
        "cfpe,cfpd->ed", attended_rows, grad_branch_all, preferred_element_type=jnp.float32
    )
    grad_heads = grad_attended.reshape(clip_count, block_count, block_rows, heads_local, HD)

    def backward_clip(members):
        clip_queries, keys, values, context_limit, clip_grads, clip_totals = members

        def backward_block(running, slices):
            key_acc, value_acc = running
            query_block, frames_block, grad_block, total_block = slices
            scores = masked_scores(query_block, keys, frames_block, context_limit)
            probability = jnp.exp(scores - total_block[..., None])
            grad_prob = jnp.einsum(
                "bhd,khd->hbk", grad_block, values, preferred_element_type=jnp.float32
            )
            inner_sum = jnp.sum(probability * grad_prob, axis=-1, keepdims=True)
            grad_scores = (probability * (grad_prob - inner_sum)).astype(jnp.bfloat16)
            grad_query = (
                jnp.einsum("hbk,khd->bhd", grad_scores, keys, preferred_element_type=jnp.float32)
                * softmax_scale
            )
            key_acc = (
                key_acc
                + jnp.einsum(
                    "hbk,bhd->khd", grad_scores, query_block, preferred_element_type=jnp.float32
                )
                * softmax_scale
            )
            value_acc = value_acc + jnp.einsum(
                "hbk,bhd->khd",
                probability.astype(jnp.bfloat16),
                grad_block,
                preferred_element_type=jnp.float32,
            )
            return ((key_acc, value_acc), grad_query.astype(jnp.bfloat16))

        empty_acc = jnp.zeros((key_rows, heads_local, HD), jnp.float32)
        (grad_keys, grad_values), grad_queries = lax.scan(
            backward_block,
            (empty_acc, empty_acc),
            (clip_queries, query_frames, clip_grads, clip_totals),
        )
        return (grad_queries, grad_keys, grad_values)

    grad_queries, grad_keys, grad_values = lax.map(
        backward_clip, (query_heads, key_heads, value_heads, context_frames, grad_heads, log_total)
    )
    key_shape = (clip_count, key_clip.shape[1], patches_all, head_cols)
    grad_key_own, grad_value_own = (
        lax.psum_scatter(
            grad_keys.reshape(key_shape).astype(jnp.bfloat16),
            "seq",
            scatter_dimension=1,
            tiled=True,
        ).astype(jnp.float32),
        lax.psum_scatter(
            grad_values.reshape(key_shape).astype(jnp.bfloat16),
            "seq",
            scatter_dimension=1,
            tiled=True,
        ).astype(jnp.float32),
    )
    grad_qkv = jnp.stack(
        [
            grad_queries.reshape(clip_count, half_frames, patches_all, head_cols),
            grad_key_own.astype(jnp.bfloat16),
            grad_value_own.astype(jnp.bfloat16),
        ],
        axis=3,
    )
    grad_w_qkv = jnp.einsum(
        "cfpd,cfpke->dke", attn_all, grad_qkv, preferred_element_type=jnp.float32
    )
    grad_qv_bias = jnp.sum(grad_qkv[:, :, :, 0::2, :].astype(jnp.float32), axis=(0, 1, 2))
    portion = grad_qkv
    grad_attn_rows = lax.psum_scatter(
        jnp.einsum("cfpke,dke->pcfd", portion, w_qkv, preferred_element_type=jnp.float32).astype(
            jnp.bfloat16
        ),
        "tensor",
        scatter_dimension=0,
        tiled=True,
    ).astype(jnp.float32)
    grad_attn_in = jnp.transpose(grad_attn_rows, (1, 2, 0, 3))
    grad_shift_one = jnp.sum(grad_attn_in, axis=2)
    grad_scale_one = jnp.sum(grad_attn_in * normed_one, axis=2)
    grad_input = grad_hidden + norm_back(grad_attn_in * (1.0 + scale_one), normed_one, inverse_one)
    grad_modulation = jnp.concatenate(
        [
            grad_shift_one,
            grad_scale_one,
            grad_gate_one,
            grad_shift_two,
            grad_scale_two,
            grad_gate_two,
        ],
        axis=-1,
    )
    grad_modulation = grad_modulation.reshape(clip_count * half_frames, 6 * breadth)
    modulation_cols, out_bias_part, down_bias_part = (
        lax.psum_scatter(
            grad_modulation.astype(jnp.bfloat16), "tensor", scatter_dimension=1, tiled=True
        ).astype(jnp.float32),
        lax.psum_scatter(
            grad_b_out.astype(jnp.bfloat16), "tensor", scatter_dimension=0, tiled=True
        ).astype(jnp.float32),
        lax.psum_scatter(
            grad_b_down.astype(jnp.bfloat16), "tensor", scatter_dimension=0, tiled=True
        ).astype(jnp.float32),
    )
    condition_rows = condition.reshape(clip_count * half_frames, breadth).astype(jnp.float32)
    grad_w_mod = jnp.dot(condition_rows.T, modulation_cols, precision=lax.Precision.HIGHEST)
    grad_b_mod = jnp.sum(modulation_cols, axis=0)
    (
        total_w_qkv,
        total_qv_bias,
        total_w_out,
        total_b_out,
        total_w_up,
        total_b_up,
        total_w_down,
        total_b_down,
        total_w_mod,
        total_b_mod,
    ) = (
        lax.psum(grad_w_qkv.astype(jnp.bfloat16), ("dp", "seq")).astype(jnp.float32),
        lax.psum(grad_qv_bias.astype(jnp.bfloat16), ("dp", "seq")).astype(jnp.float32),
        lax.psum(grad_w_out.astype(jnp.bfloat16), ("dp", "seq")).astype(jnp.float32),
        lax.psum(out_bias_part.astype(jnp.bfloat16), ("dp", "seq")).astype(jnp.float32),
        lax.psum(grad_w_up.astype(jnp.bfloat16), ("dp", "seq")).astype(jnp.float32),
        lax.psum(grad_b_up.astype(jnp.bfloat16), ("dp", "seq")).astype(jnp.float32),
        lax.psum(grad_w_down.astype(jnp.bfloat16), ("dp", "seq")).astype(jnp.float32),
        lax.psum(down_bias_part.astype(jnp.bfloat16), ("dp", "seq")).astype(jnp.float32),
        lax.psum(grad_w_mod.astype(jnp.bfloat16), ("dp", "seq")).astype(jnp.float32),
        lax.psum(grad_b_mod.astype(jnp.bfloat16), ("dp", "seq")).astype(jnp.float32),
    )
    return (
        output,
        grad_input,
        total_w_qkv,
        total_qv_bias,
        total_w_out,
        total_b_out,
        total_w_up,
        total_b_up,
        total_w_down,
        total_b_down,
        total_w_mod,
        total_b_mod,
    )


def solution(mesh):
    placed = (
        P("dp", "seq", "tensor", None),
        P(None, None, "tensor"),
        P(None, "tensor"),
        P("tensor", None),
        P(),
        P(None, "tensor"),
        P("tensor"),
        P("tensor", None),
        P(),
        P(),
        P(),
        P("dp"),
        P("dp", "seq"),
        P("dp", "seq", "tensor", None),
    )
    return jax.shard_map(
        body,
        mesh=mesh,
        in_specs=placed,
        out_specs=(
            P("dp", "seq", "tensor", None),
            P("dp", "seq", "tensor", None),
            P(None, None, "tensor"),
            P(None, "tensor"),
            P("tensor", None),
            P("tensor"),
            P(None, "tensor"),
            P("tensor"),
            P("tensor", None),
            P("tensor"),
            P(None, "tensor"),
            P("tensor"),
        ),
        check_vma=False,
    )
```

profile of v0, /device:TPU:0, one launch (start us, length us, event | category | flops | bytes accessed | tf_op | source)
XLA Modules:
  0.0 1632.9 jit_solution(15091767421687436867)
XLA Ops:
  21.3 83.5 %all-gather.8.cloned.1.call-done = bf16[1,8,256,1024]{3,2,1,0:T(8,128)(2,1)} async-done(((bf16[1,8,64,1024]{3,2,1,0:T(8,128)(2,1)}), bf16[1,8,256,1024]{3,2,1,0:T(8,128)(2,1)}) %all-gather.8.cloned.1.call-update) | async-done | bytes 4194320 | tf_op jit(solution)/shard_map/all_gather | solution.py:69
  147.6 198.6 %while.50 = (s32[]{:T(128)}, bf16[4,512,4,64]{1,3,2,0:T(8,128)(2,1)S(1)}, f32[4,4,512]{2,1,0:T(4,128)S(1)}, s32[4,512]{1,0:T(4,128)S(1)}, s32[]{:T(128)}, /*inde...) while((s32[]{:T(128)}, ...), condition=%wide.region_5.6_spmd.clone.clone, body=%wide.region_2.5_spmd.clone.clone.sunk | while | flops 2252539904 | bytes 122271888 | solution.py:116
  354.7 76.7 %reduce-scatter.8.cloned.1.call-done = bf16[64,1,8,1024]{3,0,2,1:T(8,128)(2,1)} async-done(((bf16[256,1,8,1024]{3,0,2,1:T(8,128)(2,1)}), bf16[64,1,8,1024]{3,0,2,1:T(8,128)(2,1)}) %reduce-scatter.8.cloned.1.call-update) | async-done | bytes 1048592 | tf_op jit(solution)/shard_map/reduce_scatter | solution.py:123
  436.6 81.3 %all-gather.12.cloned.1.call-done = bf16[1,8,256,1024]{3,2,1,0:T(8,128)(2,1)} async-done(((bf16[1,8,64,1024]{3,2,1,0:T(8,128)(2,1)}), bf16[1,8,256,1024]{3,2,1,0:T(8,128)(2,1)}) %all-gather.12.cloned.1.call-update) | async-done | bytes 4194320 | tf_op jit(solution)/shard_map/all_gather | solution.py:135
  535.7 74.8 %reduce-scatter.10.cloned.1.call-done = bf16[64,1,8,1024]{3,0,2,1:T(8,128)(2,1)} async-done(((bf16[256,1,8,1024]{3,0,2,1:T(8,128)(2,1)}), bf16[64,1,8,1024]{3,0,2,1:T(8,128)(2,1)}) %reduce-scatter.10.cloned.1.call-update) | async-done | bytes 1048592 | tf_op jit(solution)/shard_map/reduce_scatter | solution.py:141
  614.5 81.4 %all-gather.14.cloned.1.call-done = bf16[1,8,256,1024]{3,2,1,0:T(8,128)(2,1)} async-done(((bf16[1,8,64,1024]{3,2,1,0:T(8,128)(2,1)}), bf16[1,8,256,1024]{3,2,1,0:T(8,128)(2,1)}) %all-gather.14.cloned.1.call-update) | async-done | bytes 4194320 | tf_op jit(solution)/shard_map/all_gather | solution.py:155
  717.5 75.4 %reduce-scatter.12.cloned.1.call-done = bf16[64,1,8,1024]{3,0,2,1:T(8,128)(2,1)} async-done(((bf16[256,1,8,1024]{3,0,2,1:T(8,128)(2,1)}), bf16[64,1,8,1024]{3,0,2,1:T(8,128)(2,1)}) %reduce-scatter.12.cloned.1.call-update) | async-done | bytes 1048592 | tf_op jit(solution)/shard_map/reduce_scatter | solution.py:164
  803.0 81.3 %all-gather.16.cloned.1.call-done = bf16[1,8,256,1024]{3,2,1,0:T(8,128)(2,1)} async-done(((bf16[1,8,64,1024]{3,2,1,0:T(8,128)(2,1)}), bf16[1,8,256,1024]{3,2,1,0:T(8,128)(2,1)}) %all-gather.16.cloned.1.call-update) | async-done | bytes 4194320 | tf_op jit(solution)/shard_map/all_gather | solution.py:179
  892.2 435.7 %while.51 = (s32[]{:T(128)}, f32[4096,4,64]{0,2,1:T(8,128)}, f32[4096,4,64]{0,2,1:T(8,128)}, bf16[4,512,4,64]{1,3,2,0:T(8,128)(2,1)}, bf16[4,512,4,64]{1,3,2,0:T...) while((s32[]{:T(128)}, f32[4096,4,64]{0,2,1:T(8,128)}, ...), condition=%wide.region_15.16_spmd.clone.clone, body=%wide.region_13.15_spmd.clone.clone.sunk | while | flops 5504305152 | bytes 351639744 | solution.py:221
  928.4 25.9 %multiply_reduce_fusion.6 = (f32[4,512]{1,0:T(4,128)S(1)}, f32[4,512,4096]{2,1,0:T(8,128)}) fusion(f32[4,512,4096]{2,1,0:T(8,128)} %fusion.188, f32[4,512]{1,0:T(4,128)S(1)} %dynamic-slice_bitcast_fusion.2, pred[512,4096]{1,0:T(8,128)(4,1)S(1)} %compare_or_fusion.5, bf16[4096,4,64]{0,2,1:T(8,128)(2,1)} %get-tuple-element.648, ...), kind=kOutput, calls=%fused_computation.29.clone.1 | convolution fusion | flops 1115682816 | bytes 71581696 | tf_op jit(solution)/shard_map/while/body/eval_jaxpr/while/body/eval_jaxpr/bhd,khd->hbk/dot_general | solution.py:196
  954.3 27.6 %multiply_convert_fusion.10 = bf16[4,512,4096]{2,1,0:T(8,128)(2,1)} fusion(f32[4,512,4096]{2,1,0:T(8,128)} %get-tuple-element.583, f32[4,512,4096]{2,1,0:T(8,128)} %fusion.188, f32[4,512]{1,0:T(4,128)S(1)} %get-tuple-element.584, f32[4,512]{1,0:T(4,128)S(1)} %dynamic-slice_bitcast_fusion.2, pred[512,4096]{1,0:T(8,128)(4,1)S(1)} %compare_or_fusion.5), kind=kLoop, calls=%fused_computation.28.clone.1 | loop fusion | flops 50331648 | bytes 85999616 | tf_op jit(solution)/shard_map/while/body/eval_jaxpr/while/body/eval_jaxpr/convert_element_type | solution.py:200
  1001.5 17.3 %fusion.188 = f32[4,512,4096]{2,1,0:T(8,128)} fusion(bf16[4096,4,64]{0,2,1:T(8,128)(2,1)} %get-tuple-element.645, bf16[4,512,4,64]{1,3,2,0:T(8,128)(2,1)} %get-tuple-element.642, s32[]{:T(128)S(6)} %copy.131), kind=kOutput, calls=%fused_computation.48.clone.1 | convolution fusion | flops 1073741824 | bytes 35913732 | tf_op jit(solution)/shard_map/while/body/eval_jaxpr/while/body/eval_jaxpr/bhd,khd->hbk/dot_general | solution.py:93
  1018.8 17.7 %fusion.190 = f32[4096,4,64]{0,2,1:T(8,128)} fusion(f32[4,512,4096]{2,1,0:T(8,128)} %fusion.188, f32[4,512]{1,0:T(4,128)S(1)} %dynamic-slice_bitcast_fusion.2, pred[512,4096]{1,0:T(8,128)(4,1)S(1)} %compare_or_fusion.5, f32[4096,4,64]{0,2,1:T(8,128)} %get-tuple-element.627, pred[]{:T(512)S(6)} %compare.9, ...), kind=kOutput, calls=%fused_computation.39.clone.1 | convolution fusion | flops 1109393408 | bytes 44310532 | tf_op jit(solution)/shard_map/while/body/eval_jaxpr/while/body/eval_jaxpr/hbk,bhd->khd/dot_general | solution.py:212
  1036.5 25.9 %multiply_reduce_fusion.6 = (f32[4,512]{1,0:T(4,128)S(1)}, f32[4,512,4096]{2,1,0:T(8,128)}) fusion(f32[4,512,4096]{2,1,0:T(8,128)} %fusion.188, f32[4,512]{1,0:T(4,128)S(1)} %dynamic-slice_bitcast_fusion.2, pred[512,4096]{1,0:T(8,128)(4,1)S(1)} %compare_or_fusion.5, bf16[4096,4,64]{0,2,1:T(8,128)(2,1)} %get-tuple-element.648, ...), kind=kOutput, calls=%fused_computation.29.clone.1 | convolution fusion | flops 1115682816 | bytes 71581696 | tf_op jit(solution)/shard_map/while/body/eval_jaxpr/while/body/eval_jaxpr/bhd,khd->hbk/dot_general | solution.py:196
  1062.4 27.6 %multiply_convert_fusion.10 = bf16[4,512,4096]{2,1,0:T(8,128)(2,1)} fusion(f32[4,512,4096]{2,1,0:T(8,128)} %get-tuple-element.583, f32[4,512,4096]{2,1,0:T(8,128)} %fusion.188, f32[4,512]{1,0:T(4,128)S(1)} %get-tuple-element.584, f32[4,512]{1,0:T(4,128)S(1)} %dynamic-slice_bitcast_fusion.2, pred[512,4096]{1,0:T(8,128)(4,1)S(1)} %compare_or_fusion.5), kind=kLoop, calls=%fused_computation.28.clone.1 | loop fusion | flops 50331648 | bytes 85999616 | tf_op jit(solution)/shard_map/while/body/eval_jaxpr/while/body/eval_jaxpr/convert_element_type | solution.py:200
  1110.9 17.3 %fusion.188 = f32[4,512,4096]{2,1,0:T(8,128)} fusion(bf16[4096,4,64]{0,2,1:T(8,128)(2,1)} %get-tuple-element.645, bf16[4,512,4,64]{1,3,2,0:T(8,128)(2,1)} %get-tuple-element.642, s32[]{:T(128)S(6)} %copy.131), kind=kOutput, calls=%fused_computation.48.clone.1 | convolution fusion | flops 1073741824 | bytes 35913732 | tf_op jit(solution)/shard_map/while/body/eval_jaxpr/while/body/eval_jaxpr/bhd,khd->hbk/dot_general | solution.py:93
  1128.2 17.7 %fusion.190 = f32[4096,4,64]{0,2,1:T(8,128)} fusion(f32[4,512,4096]{2,1,0:T(8,128)} %fusion.188, f32[4,512]{1,0:T(4,128)S(1)} %dynamic-slice_bitcast_fusion.2, pred[512,4096]{1,0:T(8,128)(4,1)S(1)} %compare_or_fusion.5, f32[4096,4,64]{0,2,1:T(8,128)} %get-tuple-element.627, pred[]{:T(512)S(6)} %compare.9, ...), kind=kOutput, calls=%fused_computation.39.clone.1 | convolution fusion | flops 1109393408 | bytes 44310532 | tf_op jit(solution)/shard_map/while/body/eval_jaxpr/while/body/eval_jaxpr/hbk,bhd->khd/dot_general | solution.py:212
  1145.9 25.9 %multiply_reduce_fusion.6 = (f32[4,512]{1,0:T(4,128)S(1)}, f32[4,512,4096]{2,1,0:T(8,128)}) fusion(f32[4,512,4096]{2,1,0:T(8,128)} %fusion.188, f32[4,512]{1,0:T(4,128)S(1)} %dynamic-slice_bitcast_fusion.2, pred[512,4096]{1,0:T(8,128)(4,1)S(1)} %compare_or_fusion.5, bf16[4096,4,64]{0,2,1:T(8,128)(2,1)} %get-tuple-element.648, ...), kind=kOutput, calls=%fused_computation.29.clone.1 | convolution fusion | flops 1115682816 | bytes 71581696 | tf_op jit(solution)/shard_map/while/body/eval_jaxpr/while/body/eval_jaxpr/bhd,khd->hbk/dot_general | solution.py:196
  1171.8 27.6 %multiply_convert_fusion.10 = bf16[4,512,4096]{2,1,0:T(8,128)(2,1)} fusion(f32[4,512,4096]{2,1,0:T(8,128)} %get-tuple-element.583, f32[4,512,4096]{2,1,0:T(8,128)} %fusion.188, f32[4,512]{1,0:T(4,128)S(1)} %get-tuple-element.584, f32[4,512]{1,0:T(4,128)S(1)} %dynamic-slice_bitcast_fusion.2, pred[512,4096]{1,0:T(8,128)(4,1)S(1)} %compare_or_fusion.5), kind=kLoop, calls=%fused_computation.28.clone.1 | loop fusion | flops 50331648 | bytes 85999616 | tf_op jit(solution)/shard_map/while/body/eval_jaxpr/while/body/eval_jaxpr/convert_element_type | solution.py:200
  1237.6 17.7 %fusion.190 = f32[4096,4,64]{0,2,1:T(8,128)} fusion(f32[4,512,4096]{2,1,0:T(8,128)} %fusion.188, f32[4,512]{1,0:T(4,128)S(1)} %dynamic-slice_bitcast_fusion.2, pred[512,4096]{1,0:T(8,128)(4,1)S(1)} %compare_or_fusion.5, f32[4096,4,64]{0,2,1:T(8,128)} %get-tuple-element.627, pred[]{:T(512)S(6)} %compare.9, ...), kind=kOutput, calls=%fused_computation.39.clone.1 | convolution fusion | flops 1109393408 | bytes 44310532 | tf_op jit(solution)/shard_map/while/body/eval_jaxpr/while/body/eval_jaxpr/hbk,bhd->khd/dot_general | solution.py:212
  1255.3 25.9 %multiply_reduce_fusion.6 = (f32[4,512]{1,0:T(4,128)S(1)}, f32[4,512,4096]{2,1,0:T(8,128)}) fusion(f32[4,512,4096]{2,1,0:T(8,128)} %fusion.188, f32[4,512]{1,0:T(4,128)S(1)} %dynamic-slice_bitcast_fusion.2, pred[512,4096]{1,0:T(8,128)(4,1)S(1)} %compare_or_fusion.5, bf16[4096,4,64]{0,2,1:T(8,128)(2,1)} %get-tuple-element.648, ...), kind=kOutput, calls=%fused_computation.29.clone.1 | convolution fusion | flops 1115682816 | bytes 71581696 | tf_op jit(solution)/shard_map/while/body/eval_jaxpr/while/body/eval_jaxpr/bhd,khd->hbk/dot_general | solution.py:196
  1281.2 27.6 %multiply_convert_fusion.10 = bf16[4,512,4096]{2,1,0:T(8,128)(2,1)} fusion(f32[4,512,4096]{2,1,0:T(8,128)} %get-tuple-element.583, f32[4,512,4096]{2,1,0:T(8,128)} %fusion.188, f32[4,512]{1,0:T(4,128)S(1)} %get-tuple-element.584, f32[4,512]{1,0:T(4,128)S(1)} %dynamic-slice_bitcast_fusion.2, pred[512,4096]{1,0:T(8,128)(4,1)S(1)} %compare_or_fusion.5), kind=kLoop, calls=%fused_computation.28.clone.1 | loop fusion | flops 50331648 | bytes 85999616 | tf_op jit(solution)/shard_map/while/body/eval_jaxpr/while/body/eval_jaxpr/convert_element_type | solution.py:200
  1389.7 55.0 %reduce-scatter.18.cloned.1.call-done = bf16[64,1,8,1024]{3,0,2,1:T(8,128)(2,1)} async-done(((bf16[256,1,8,1024]{3,0,2,1:T(8,128)(2,1)}), bf16[64,1,8,1024]{3,0,2,1:T(8,128)(2,1)}) %reduce-scatter.18.cloned.1.call-update) | async-done | bytes 1048592 | tf_op jit(solution)/shard_map/reduce_scatter | solution.py:259
  1504.7 106.7 %all-reduce.7.cloned.1.call-done = (bf16[1024,3,256]{2,0,1:T(8,128)(2,1)}, bf16[256,1024]{1,0:T(8,128)(2,1)}, bf16[1024,1024]{1,0:T(8,128)(2,1)}, bf16[1024,1024]{1,0:T(8,128)(2,1)}, bf16[1024,1536]{1,0:T(8,128)(2,1)}) async-done(((bf16[1024,3,256]{2,0,1:T(8,128)(2,1)}, bf16[256,1024]{1,0:T(8,128)(2,1)}, bf16[1024,1024]{1,0:T(8,128)(2,1)}, bf16[1024,1024]{1,0:T(8,128)(2,1)}, bf16[1024,1536]{1,0:T(8,128)(2,1)}), ...) | async-done | bytes 9437200 | tf_op jit(solution)/shard_map/psum | solution.py:309
  (324 shorter events, 597.2 us)
Async XLA Ops:
  7.2 520.9 %copy-start = (bf16[1024,1024]{1,0:T(8,128)(2,1)S(1)}, bf16[1024,1024]{1,0:T(8,128)(2,1)}, u32[]{:S(2)}) copy-start(bf16[1024,1024]{1,0:T(8,128)(2,1)} %param.25) | copy-start | bytes 6291460
  7.2 97.7 %all-gather.8.cloned.1.call-start = ((), (), s32[]{:S(2)}) async-start(), calls=%async_computation.7 | async-start | bytes 5242880 | tf_op jit(solution)/shard_map/all_gather | solution.py:69
  21.3 108.8 %all-gather.10.cloned.1.call-start = ((), (), s32[]{:S(2)}) async-start(), calls=%async_computation.8 | async-start | bytes 3145728 | tf_op jit(solution)/shard_map/all_gather | solution.py:77
  114.4 24.4 %all-gather.18.cloned.1.call-start = ((), (), s32[]{:S(2)}) async-start(), calls=%async_computation.19 | async-start | bytes 3145728 | tf_op jit(solution)/shard_map/all_gather | solution.py:76
  117.2 314.2 %reduce-scatter.8.cloned.1.call-start = ((), (), s32[]{:S(2)}) async-start(), calls=%async_computation.9 | async-start | bytes 5242880 | tf_op jit(solution)/shard_map/reduce_scatter | solution.py:123
  349.8 81.6 %copy-start.23 = (f32[8,1024]{1,0:T(8,128)S(1)}, f32[8,1024]{1,0:T(8,128)}, u32[]{:S(2)}) copy-start(f32[8,1024]{1,0:T(8,128)} %get-tuple-element.454) | copy-start | bytes 98308
  354.6 80.4 %copy-start.24 = (f32[8,1024]{1,0:T(8,128)S(1)}, f32[8,1024]{1,0:T(8,128)}, u32[]{:S(2)}) copy-start(f32[8,1024]{1,0:T(8,128)} %get-tuple-element.451) | copy-start | bytes 98308
  354.6 80.4 %copy-start.32 = (f32[8,1024]{1,0:T(8,128)S(1)}, f32[8,1024]{1,0:T(8,128)}, u32[]{:S(2)}) copy-start(f32[8,1024]{1,0:T(8,128)} %get-tuple-element.450) | copy-start | bytes 98308
  354.6 163.3 %all-gather.12.cloned.1.call-start = ((), (), s32[]{:S(2)}) async-start(), calls=%async_computation.10 | async-start | bytes 5242880 | tf_op jit(solution)/shard_map/all_gather | solution.py:135
  436.5 174.0 %reduce-scatter.10.cloned.1.call-start = ((), (), s32[]{:S(2)}) async-start(), calls=%async_computation.11 | async-start | bytes 5242880 | tf_op jit(solution)/shard_map/reduce_scatter | solution.py:141
  436.6 259.3 %copy-start.45 = (f32[1024]{0:T(1024)}, f32[1024]{0:T(1024)S(1)}, u32[]{:S(2)}) copy-start(f32[1024]{0:T(1024)S(1)} %convert_element_type.268) | copy-start | bytes 12292
  535.0 75.5 %copy-start.26 = (f32[8,1024]{1,0:T(8,128)S(1)}, f32[8,1024]{1,0:T(8,128)}, u32[]{:S(2)}) copy-start(f32[8,1024]{1,0:T(8,128)} %get-tuple-element.449) | copy-start | bytes 98308
  535.1 160.8 %all-gather.14.cloned.1.call-start = ((), (), s32[]{:S(2)}) async-start(), calls=%async_computation.12 | async-start | bytes 5242880 | tf_op jit(solution)/shard_map/all_gather | solution.py:155
  614.4 178.5 %reduce-scatter.12.cloned.1.call-start = ((), (), s32[]{:S(2)}) async-start(), calls=%async_computation.13 | async-start | bytes 5242880 | tf_op jit(solution)/shard_map/reduce_scatter | solution.py:164
  717.4 75.5 %copy-start.7 = (f32[1,8,64,1024]{3,2,1,0:T(8,128)S(1)}, f32[1,8,64,1024]{3,2,1,0:T(8,128)}, u32[]{:S(2)}) copy-start(f32[1,8,64,1024]{3,2,1,0:T(8,128)} %copy-done.6) | copy-start | bytes 6291460
  717.4 78.4 %copy-start.17 = (bf16[64,1,8,1024]{3,0,2,1:T(8,128)(2,1)S(1)}, bf16[64,1,8,1024]{3,0,2,1:T(8,128)(2,1)}, u32[]{:S(2)}) copy-start(bf16[64,1,8,1024]{3,0,2,1:T(8,128)(2,1)} %reduce-scatter.8.cloned.1.call-done) | copy-start | bytes 3145732
  717.5 166.9 %all-gather.16.cloned.1.call-start = ((), (), s32[]{:S(2)}) async-start(), calls=%async_computation.14 | async-start | bytes 5242880 | tf_op jit(solution)/shard_map/all_gather | solution.py:179
  800.4 84.0 %copy-start.25 = (bf16[256,1024]{1,0:T(8,128)(2,1)S(1)}, bf16[256,1024]{1,0:T(8,128)(2,1)}, u32[]{:S(2)}) copy-start(bf16[256,1024]{1,0:T(8,128)(2,1)} %param.21) | copy-start | bytes 1572868
  803.0 545.5 %reduce-scatter.14.cloned.1.call-start = ((), (), s32[]{:S(2)}) async-start(), calls=%async_computation.15 | async-start | bytes 3145728 | tf_op jit(solution)/shard_map/reduce_scatter | solution.py:233
  1336.7 22.3 %reduce-scatter.16.cloned.1.call-start = ((), (), s32[]{:S(2)}) async-start(), calls=%async_computation.16 | async-start | bytes 3145728 | tf_op jit(solution)/shard_map/reduce_scatter | solution.py:239
  1345.6 99.1 %reduce-scatter.18.cloned.1.call-start = ((), (), s32[]{:S(2)}) async-start(), calls=%async_computation.17 | async-start | bytes 5242880 | tf_op jit(solution)/shard_map/reduce_scatter | solution.py:259
  1366.6 102.9 %reduce-scatter.20.cloned.1.call-start = ((), (), s32[]{:S(2)}) async-start(), calls=%async_computation.18 | async-start | bytes 122880 | tf_op jit(solution)/shard_map/reduce_scatter | solution.py:284
  1389.7 59.0 %copy-start.38 = (bf16[8,1024]{1,0:T(8,128)(2,1)S(1)}, bf16[8,1024]{1,0:T(8,128)(2,1)}, u32[]{:S(2)}) copy-start(bf16[8,1024]{1,0:T(8,128)(2,1)} %get-tuple-element.384) | copy-start | bytes 49156
  1449.5 161.9 %all-reduce.7.cloned.1.call-start = ((), (), s32[]{:S(2)}) async-start(), calls=%async_computation.20 | async-start | bytes 18874368 | tf_op jit(solution)/shard_map/psum | solution.py:309
  (54 other events, 681.1 us)
Sparse Core Ops, SparseCore 0:
  21.4 83.4 all-gather.7
  114.6 9.0 all-gather.9
  125.8 11.7 all-gather.17
  354.7 76.6 reduce-scatter.7
  436.6 81.2 all-gather.11
  535.2 75.2 reduce-scatter.9
  614.6 81.2 all-gather.13
  717.6 75.2 reduce-scatter.11
  803.1 81.2 all-gather.15
  1336.8 8.2 reduce-scatter.13
  1347.9 11.0 reduce-scatter.15
  1366.7 78.0 reduce-scatter.17
  1449.6 19.8 reduce-scatter.19
  1474.8 136.5 all-reduce.6
where the time goes:
time: 1640 us; the launch traced here: 1630 us
  waiting for transfers between devices  739 us (45%)
  matrix products  536 us (33%)
  other arithmetic  244 us (15%)
  local copies, waits for them, and re-layouts  73.1 us (4%)
  blocking collectives  22.1 us (1%)
  between operations  16.4 us (1%)
    dot_general x8, matrix products, masked_scores(): jnp.einsum('bhd,khd->hbk', query_block, keys, preferred_element_type=jnp....  133 us
    convert_element_type x4, other arithmetic, backward_block(): grad_scores = (probability * (grad_prob - inner_sum)).astype(jnp.bfloat16)  110 us
    psum x1, waiting for transfers between devices, body(): lax.psum(grad_w_qkv.astype(jnp.bfloat16), ('dp', 'seq')).astype(jnp.float32)  107 us
    dot_general x4, matrix products, backward_block(): jnp.einsum('bhd,khd->hbk', grad_block, values, preferred_element_type=jnp...  104 us
    all_gather x1, waiting for transfers between devices, body(): attn_all = lax.all_gather(attn_in, 'tensor', axis=2, tiled=True)  83.5 us
    all_gather x1, waiting for transfers between devices, body(): grad_mlp_all = lax.all_gather(grad_mlp_low, 'tensor', axis=2, tiled=True)  81.4 us
    all_gather x1, waiting for transfers between devices, body(): mlp_all = lax.all_gather(mlp_in, 'tensor', axis=2, tiled=True)  81.3 us
    all_gather x1, waiting for transfers between devices, body(): lax.all_gather(grad_branch.astype(jnp.bfloat16), 'tensor', axis=2, tiled=...  81.3 us
  transfers between devices with their start and end apart: 14, of which 11 were waited for; matrix products, arithmetic and copies ran while one was open for 5% of the time, Pallas kernels for 0%

commit v1 on v0

--- a/solution.py
+++ b/solution.py
@@ -5,6 +5,26 @@
 from jax.sharding import PartitionSpec as P
 
 HD = 64
+
+
+def number_surface_on(local_array):
+    parts_n = lax.axis_size("tensor")
+    ledger = []
+    for at in range(parts_n):
+        ledger.append((at, (at + 1) % parts_n))
+    slots = []
+    for at in range(parts_n):
+        slots.append((at, (at - 1) % parts_n))
+    all_values, high = ([local_array], [local_array])
+    for _ in range(parts_n // 2):
+        mixed_arr = lax.ppermute(all_values[-1], "tensor", ledger)
+        all_values.append(mixed_arr)
+    for _ in range((parts_n - 1) // 2):
+        part_next = lax.ppermute(high[-1], "tensor", slots)
+        high.append(part_next)
+    formed = jnp.concatenate([*all_values[::-1], *high[1:]], 2)
+    arr_out = lax.axis_index("tensor")
+    return jnp.roll(formed, (arr_out - parts_n // 2) * local_array.shape[2], axis=2)
 
 
 def level_features(levels, context, frame_ids, breadth):
@@ -132,7 +152,7 @@
     hidden_one = block_input + gate_one * branch_one
     normed_two, inverse_two = normalize(hidden_one)
     mlp_in = (normed_two * (1.0 + scale_two) + shift_two).astype(jnp.bfloat16)
-    mlp_all = lax.all_gather(mlp_in, "tensor", axis=2, tiled=True)
+    mlp_all = number_surface_on(mlp_in)
     pre_act = jnp.einsum(
         "cfpd,de->cfpe", mlp_all, w_up, preferred_element_type=jnp.float32
     ) + b_up.astype(jnp.float32)

time: 1640 us -> 1640 us (level)
    all_gather x1 -> x0, waiting for transfers between devices: 81.3 us -> none  [body(): mlp_all = lax.all_gather(mlp_in, 'tensor', axis=2, tiled=True)]
    ppermute x0 -> x3, waiting for transfers between devices: none -> 66.1 us  [the longest x2 49.2 us: number_surface_on(): mixed_arr = lax.ppermute(all_values[-1], 'tensor', ledger)]
  transfers between devices with their start and end apart: 14 -> 16, of which waited for: 11 -> 13; matrix products, arithmetic and copies ran while one was open for 5% -> 5% of each run, Pallas kernels for 0% -> 0%
where the time goes in v1:
time: 1640 us; the launch traced here: 1630 us
  waiting for transfers between devices  726 us (44%)
  matrix products  534 us (33%)
  other arithmetic  245 us (15%)
  local copies, waits for them, and re-layouts  81.6 us (5%)
  blocking collectives  22.1 us (1%)
  between operations  16.4 us (1%)
    dot_general x8, matrix products, masked_scores(): jnp.einsum('bhd,khd->hbk', query_block, keys, preferred_element_type=jnp....  133 us
    convert_element_type x4, other arithmetic, backward_block(): grad_scores = (probability * (grad_prob - inner_sum)).astype(jnp.bfloat16)  111 us
    psum x1, waiting for transfers between devices, body(): lax.psum(grad_w_qkv.astype(jnp.bfloat16), ('dp', 'seq')).astype(jnp.float32)  107 us
    dot_general x4, matrix products, backward_block(): jnp.einsum('bhd,khd->hbk', grad_block, values, preferred_element_type=jnp...  104 us
    all_gather x1, waiting for transfers between devices, body(): attn_all = lax.all_gather(attn_in, 'tensor', axis=2, tiled=True)  83.5 us
    all_gather x1, waiting for transfers between devices, body(): grad_mlp_all = lax.all_gather(grad_mlp_low, 'tensor', axis=2, tiled=True)  81.4 us
    all_gather x1, waiting for transfers between devices, body(): lax.all_gather(grad_branch.astype(jnp.bfloat16), 'tensor', axis=2, tiled=...  81.3 us
    reduce_scatter x1, waiting for transfers between devices, body(): lax.psum_scatter(jnp.einsum('cfpe,ed->pcfd', portion, w_down, preferred_e...  77 us
  transfers between devices with their start and end apart: 16, of which 13 were waited for; matrix products, arithmetic and copies ran while one was open for 5% of the time, Pallas kernels for 0%

profile of v1, /device:TPU:0, one launch (start us, length us, event | category | flops | bytes accessed | tf_op | source)
XLA Modules:
  0.0 1632.6 jit_solution(8587661015781453267)
XLA Ops:
  21.3 83.5 %all-gather.7.cloned.1.call-done = bf16[1,8,256,1024]{3,2,1,0:T(8,128)(2,1)} async-done(((bf16[1,8,64,1024]{3,2,1,0:T(8,128)(2,1)}), bf16[1,8,256,1024]{3,2,1,0:T(8,128)(2,1)}) %all-gather.7.cloned.1.call-update) | async-done | bytes 4194320 | tf_op jit(solution)/shard_map/all_gather | solution.py:89
  147.6 198.1 %while.50 = (s32[]{:T(128)}, bf16[4,512,4,64]{1,3,2,0:T(8,128)(2,1)S(1)}, f32[4,4,512]{2,1,0:T(4,128)S(1)}, s32[4,512]{1,0:T(4,128)S(1)}, s32[]{:T(128)}, /*inde...) while((s32[]{:T(128)}, ...), condition=%wide.region_5.6_spmd.clone.clone, body=%wide.region_2.5_spmd.clone.clone.sunk | while | flops 2252539904 | bytes 122271888 | solution.py:136
  354.0 76.8 %reduce-scatter.8.cloned.1.call-done = bf16[64,1,8,1024]{3,0,2,1:T(8,128)(2,1)} async-done(((bf16[256,1,8,1024]{3,0,2,1:T(8,128)(2,1)}), bf16[64,1,8,1024]{3,0,2,1:T(8,128)(2,1)}) %reduce-scatter.8.cloned.1.call-update) | async-done | bytes 1048592 | tf_op jit(solution)/shard_map/reduce_scatter | solution.py:143
  437.3 25.1 %collective-permute-done = bf16[1,8,64,1024]{3,2,1,0:T(8,128)(2,1)S(1)} collective-permute-done((bf16[1,8,64,1024]{3,2,1,0:T(8,128)(2,1)}, bf16[1,8,64,1024]{3,2,1,0:T(8,128)(2,1)S(1)}, u32[]{:S(2)}, u32[]{:S(2)}) %collective-permute-start) | collective-permute-done | bytes 1048608 | tf_op jit(solution)/shard_map/ppermute | solution.py:20
  466.2 24.1 %collective-permute-done.1 = bf16[1,8,64,1024]{3,2,1,0:T(8,128)(2,1)} collective-permute-done((bf16[1,8,64,1024]{3,2,1,0:T(8,128)(2,1)S(1)}, bf16[1,8,64,1024]{3,2,1,0:T(8,128)(2,1)}, u32[]{:S(2)}, u32[]{:S(2)}) %collective-permute-start.1) | collective-permute-done | bytes 1048608 | tf_op jit(solution)/shard_map/ppermute | solution.py:20
  532.5 77.0 %reduce-scatter.10.cloned.1.call-done = bf16[64,1,8,1024]{3,0,2,1:T(8,128)(2,1)} async-done(((bf16[256,1,8,1024]{3,0,2,1:T(8,128)(2,1)}), bf16[64,1,8,1024]{3,0,2,1:T(8,128)(2,1)}) %reduce-scatter.10.cloned.1.call-update) | async-done | bytes 1048592 | tf_op jit(solution)/shard_map/reduce_scatter | solution.py:161
  613.5 81.4 %all-gather.11.cloned.1.call-done = bf16[1,8,256,1024]{3,2,1,0:T(8,128)(2,1)} async-done(((bf16[1,8,64,1024]{3,2,1,0:T(8,128)(2,1)}), bf16[1,8,256,1024]{3,2,1,0:T(8,128)(2,1)}) %all-gather.11.cloned.1.call-update) | async-done | bytes 4194320 | tf_op jit(solution)/shard_map/all_gather | solution.py:175
  717.0 75.4 %reduce-scatter.12.cloned.1.call-done = bf16[64,1,8,1024]{3,0,2,1:T(8,128)(2,1)} async-done(((bf16[256,1,8,1024]{3,0,2,1:T(8,128)(2,1)}), bf16[64,1,8,1024]{3,0,2,1:T(8,128)(2,1)}) %reduce-scatter.12.cloned.1.call-update) | async-done | bytes 1048592 | tf_op jit(solution)/shard_map/reduce_scatter | solution.py:184
  802.5 81.3 %all-gather.13.cloned.1.call-done = bf16[1,8,256,1024]{3,2,1,0:T(8,128)(2,1)} async-done(((bf16[1,8,64,1024]{3,2,1,0:T(8,128)(2,1)}), bf16[1,8,256,1024]{3,2,1,0:T(8,128)(2,1)}) %all-gather.13.cloned.1.call-update) | async-done | bytes 4194320 | tf_op jit(solution)/shard_map/all_gather | solution.py:199
  891.6 436.1 %while.51 = (s32[]{:T(128)}, f32[4096,4,64]{0,2,1:T(8,128)}, f32[4096,4,64]{0,2,1:T(8,128)}, bf16[4,512,4,64]{1,3,2,0:T(8,128)(2,1)}, bf16[4,512,4,64]{1,3,2,0:T...) while((s32[]{:T(128)}, f32[4096,4,64]{0,2,1:T(8,128)}, ...), condition=%wide.region_15.16_spmd.clone.clone, body=%wide.region_13.15_spmd.clone.clone.sunk | while | flops 5504305152 | bytes 351639744 | solution.py:241
  894.0 17.3 %fusion.192 = f32[4,512,4096]{2,1,0:T(8,128)} fusion(bf16[4096,4,64]{0,2,1:T(8,128)(2,1)} %get-tuple-element.645, bf16[4,512,4,64]{1,3,2,0:T(8,128)(2,1)} %get-tuple-element.642, s32[]{:T(128)S(6)} %copy.138), kind=kOutput, calls=%fused_computation.48.clone.1 | convolution fusion | flops 1073741824 | bytes 35913732 | tf_op jit(solution)/shard_map/while/body/eval_jaxpr/while/body/eval_jaxpr/bhd,khd->hbk/dot_general | solution.py:113
  927.8 26.0 %multiply_reduce_fusion.6 = (f32[4,512]{1,0:T(4,128)S(1)}, f32[4,512,4096]{2,1,0:T(8,128)}) fusion(f32[4,512,4096]{2,1,0:T(8,128)} %fusion.192, f32[4,512]{1,0:T(4,128)S(1)} %dynamic-slice_bitcast_fusion.2, pred[512,4096]{1,0:T(8,128)(4,1)S(1)} %compare_or_fusion.5, bf16[4096,4,64]{0,2,1:T(8,128)(2,1)} %get-tuple-element.648, ...), kind=kOutput, calls=%fused_computation.29.clone.1 | convolution fusion | flops 1115682816 | bytes 71581696 | tf_op jit(solution)/shard_map/while/body/eval_jaxpr/while/body/eval_jaxpr/bhd,khd->hbk/dot_general | solution.py:216
  953.8 27.6 %multiply_convert_fusion.10 = bf16[4,512,4096]{2,1,0:T(8,128)(2,1)} fusion(f32[4,512,4096]{2,1,0:T(8,128)} %get-tuple-element.583, f32[4,512,4096]{2,1,0:T(8,128)} %fusion.192, f32[4,512]{1,0:T(4,128)S(1)} %get-tuple-element.584, f32[4,512]{1,0:T(4,128)S(1)} %dynamic-slice_bitcast_fusion.2, pred[512,4096]{1,0:T(8,128)(4,1)S(1)} %compare_or_fusion.5), kind=kLoop, calls=%fused_computation.28.clone.1 | loop fusion | flops 50331648 | bytes 85999616 | tf_op jit(solution)/shard_map/while/body/eval_jaxpr/while/body/eval_jaxpr/convert_element_type | solution.py:220
  1018.3 17.7 %fusion.194 = f32[4096,4,64]{0,2,1:T(8,128)} fusion(f32[4,512,4096]{2,1,0:T(8,128)} %fusion.192, f32[4,512]{1,0:T(4,128)S(1)} %dynamic-slice_bitcast_fusion.2, pred[512,4096]{1,0:T(8,128)(4,1)S(1)} %compare_or_fusion.5, f32[4096,4,64]{0,2,1:T(8,128)} %get-tuple-element.627, pred[]{:T(512)S(6)} %compare.10, ...), kind=kOutput, calls=%fused_computation.39.clone.1 | convolution fusion | flops 1109393408 | bytes 44310532 | tf_op jit(solution)/shard_map/while/body/eval_jaxpr/while/body/eval_jaxpr/hbk,bhd->khd/dot_general | solution.py:232
  1036.0 26.0 %multiply_reduce_fusion.6 = (f32[4,512]{1,0:T(4,128)S(1)}, f32[4,512,4096]{2,1,0:T(8,128)}) fusion(f32[4,512,4096]{2,1,0:T(8,128)} %fusion.192, f32[4,512]{1,0:T(4,128)S(1)} %dynamic-slice_bitcast_fusion.2, pred[512,4096]{1,0:T(8,128)(4,1)S(1)} %compare_or_fusion.5, bf16[4096,4,64]{0,2,1:T(8,128)(2,1)} %get-tuple-element.648, ...), kind=kOutput, calls=%fused_computation.29.clone.1 | convolution fusion | flops 1115682816 | bytes 71581696 | tf_op jit(solution)/shard_map/while/body/eval_jaxpr/while/body/eval_jaxpr/bhd,khd->hbk/dot_general | solution.py:216
  1062.0 27.6 %multiply_convert_fusion.10 = bf16[4,512,4096]{2,1,0:T(8,128)(2,1)} fusion(f32[4,512,4096]{2,1,0:T(8,128)} %get-tuple-element.583, f32[4,512,4096]{2,1,0:T(8,128)} %fusion.192, f32[4,512]{1,0:T(4,128)S(1)} %get-tuple-element.584, f32[4,512]{1,0:T(4,128)S(1)} %dynamic-slice_bitcast_fusion.2, pred[512,4096]{1,0:T(8,128)(4,1)S(1)} %compare_or_fusion.5), kind=kLoop, calls=%fused_computation.28.clone.1 | loop fusion | flops 50331648 | bytes 85999616 | tf_op jit(solution)/shard_map/while/body/eval_jaxpr/while/body/eval_jaxpr/convert_element_type | solution.py:220
  1127.8 17.7 %fusion.194 = f32[4096,4,64]{0,2,1:T(8,128)} fusion(f32[4,512,4096]{2,1,0:T(8,128)} %fusion.192, f32[4,512]{1,0:T(4,128)S(1)} %dynamic-slice_bitcast_fusion.2, pred[512,4096]{1,0:T(8,128)(4,1)S(1)} %compare_or_fusion.5, f32[4096,4,64]{0,2,1:T(8,128)} %get-tuple-element.627, pred[]{:T(512)S(6)} %compare.10, ...), kind=kOutput, calls=%fused_computation.39.clone.1 | convolution fusion | flops 1109393408 | bytes 44310532 | tf_op jit(solution)/shard_map/while/body/eval_jaxpr/while/body/eval_jaxpr/hbk,bhd->khd/dot_general | solution.py:232
  1145.5 26.0 %multiply_reduce_fusion.6 = (f32[4,512]{1,0:T(4,128)S(1)}, f32[4,512,4096]{2,1,0:T(8,128)}) fusion(f32[4,512,4096]{2,1,0:T(8,128)} %fusion.192, f32[4,512]{1,0:T(4,128)S(1)} %dynamic-slice_bitcast_fusion.2, pred[512,4096]{1,0:T(8,128)(4,1)S(1)} %compare_or_fusion.5, bf16[4096,4,64]{0,2,1:T(8,128)(2,1)} %get-tuple-element.648, ...), kind=kOutput, calls=%fused_computation.29.clone.1 | convolution fusion | flops 1115682816 | bytes 71581696 | tf_op jit(solution)/shard_map/while/body/eval_jaxpr/while/body/eval_jaxpr/bhd,khd->hbk/dot_general | solution.py:216
  1171.5 27.6 %multiply_convert_fusion.10 = bf16[4,512,4096]{2,1,0:T(8,128)(2,1)} fusion(f32[4,512,4096]{2,1,0:T(8,128)} %get-tuple-element.583, f32[4,512,4096]{2,1,0:T(8,128)} %fusion.192, f32[4,512]{1,0:T(4,128)S(1)} %get-tuple-element.584, f32[4,512]{1,0:T(4,128)S(1)} %dynamic-slice_bitcast_fusion.2, pred[512,4096]{1,0:T(8,128)(4,1)S(1)} %compare_or_fusion.5), kind=kLoop, calls=%fused_computation.28.clone.1 | loop fusion | flops 50331648 | bytes 85999616 | tf_op jit(solution)/shard_map/while/body/eval_jaxpr/while/body/eval_jaxpr/convert_element_type | solution.py:220
  1237.3 17.7 %fusion.194 = f32[4096,4,64]{0,2,1:T(8,128)} fusion(f32[4,512,4096]{2,1,0:T(8,128)} %fusion.192, f32[4,512]{1,0:T(4,128)S(1)} %dynamic-slice_bitcast_fusion.2, pred[512,4096]{1,0:T(8,128)(4,1)S(1)} %compare_or_fusion.5, f32[4096,4,64]{0,2,1:T(8,128)} %get-tuple-element.627, pred[]{:T(512)S(6)} %compare.10, ...), kind=kOutput, calls=%fused_computation.39.clone.1 | convolution fusion | flops 1109393408 | bytes 44310532 | tf_op jit(solution)/shard_map/while/body/eval_jaxpr/while/body/eval_jaxpr/hbk,bhd->khd/dot_general | solution.py:232
  1255.0 26.0 %multiply_reduce_fusion.6 = (f32[4,512]{1,0:T(4,128)S(1)}, f32[4,512,4096]{2,1,0:T(8,128)}) fusion(f32[4,512,4096]{2,1,0:T(8,128)} %fusion.192, f32[4,512]{1,0:T(4,128)S(1)} %dynamic-slice_bitcast_fusion.2, pred[512,4096]{1,0:T(8,128)(4,1)S(1)} %compare_or_fusion.5, bf16[4096,4,64]{0,2,1:T(8,128)(2,1)} %get-tuple-element.648, ...), kind=kOutput, calls=%fused_computation.29.clone.1 | convolution fusion | flops 1115682816 | bytes 71581696 | tf_op jit(solution)/shard_map/while/body/eval_jaxpr/while/body/eval_jaxpr/bhd,khd->hbk/dot_general | solution.py:216
  1281.0 27.6 %multiply_convert_fusion.10 = bf16[4,512,4096]{2,1,0:T(8,128)(2,1)} fusion(f32[4,512,4096]{2,1,0:T(8,128)} %get-tuple-element.583, f32[4,512,4096]{2,1,0:T(8,128)} %fusion.192, f32[4,512]{1,0:T(4,128)S(1)} %get-tuple-element.584, f32[4,512]{1,0:T(4,128)S(1)} %dynamic-slice_bitcast_fusion.2, pred[512,4096]{1,0:T(8,128)(4,1)S(1)} %compare_or_fusion.5), kind=kLoop, calls=%fused_computation.28.clone.1 | loop fusion | flops 50331648 | bytes 85999616 | tf_op jit(solution)/shard_map/while/body/eval_jaxpr/while/body/eval_jaxpr/convert_element_type | solution.py:220
  1389.3 55.0 %reduce-scatter.18.cloned.1.call-done = bf16[64,1,8,1024]{3,0,2,1:T(8,128)(2,1)} async-done(((bf16[256,1,8,1024]{3,0,2,1:T(8,128)(2,1)}), bf16[64,1,8,1024]{3,0,2,1:T(8,128)(2,1)}) %reduce-scatter.18.cloned.1.call-update) | async-done | bytes 1048592 | tf_op jit(solution)/shard_map/reduce_scatter | solution.py:279
  1504.3 106.9 %all-reduce.7.cloned.1.call-done = (bf16[1024,3,256]{2,0,1:T(8,128)(2,1)}, bf16[256,1024]{1,0:T(8,128)(2,1)}, bf16[1024,1024]{1,0:T(8,128)(2,1)}, bf16[1024,1024]{1,0:T(8,128)(2,1)}, bf16[1024,1536]{1,0:T(8,128)(2,1)}) async-done(((bf16[1024,3,256]{2,0,1:T(8,128)(2,1)}, bf16[256,1024]{1,0:T(8,128)(2,1)}, bf16[1024,1024]{1,0:T(8,128)(2,1)}, bf16[1024,1024]{1,0:T(8,128)(2,1)}, bf16[1024,1536]{1,0:T(8,128)(2,1)}), ...) | async-done | bytes 9437200 | tf_op jit(solution)/shard_map/psum | solution.py:329
  (341 shorter events, 643.5 us)
Async XLA Ops:
  7.2 517.7 %copy-start = (bf16[1024,1024]{1,0:T(8,128)(2,1)S(1)}, bf16[1024,1024]{1,0:T(8,128)(2,1)}, u32[]{:S(2)}) copy-start(bf16[1024,1024]{1,0:T(8,128)(2,1)} %param.25) | copy-start | bytes 6291460
  7.2 97.7 %all-gather.7.cloned.1.call-start = ((), (), s32[]{:S(2)}) async-start(), calls=%async_computation.7 | async-start | bytes 5242880 | tf_op jit(solution)/shard_map/all_gather | solution.py:89
  21.3 108.8 %all-gather.9.cloned.1.call-start = ((), (), s32[]{:S(2)}) async-start(), calls=%async_computation.8 | async-start | bytes 3145728 | tf_op jit(solution)/shard_map/all_gather | solution.py:97
  114.4 24.4 %all-gather.15.cloned.1.call-start = ((), (), s32[]{:S(2)}) async-start(), calls=%async_computation.18 | async-start | bytes 3145728 | tf_op jit(solution)/shard_map/all_gather | solution.py:96
  117.2 313.5 %reduce-scatter.8.cloned.1.call-start = ((), (), s32[]{:S(2)}) async-start(), calls=%async_computation.9 | async-start | bytes 5242880 | tf_op jit(solution)/shard_map/reduce_scatter | solution.py:143
  349.0 81.7 %copy-start.25 = (f32[8,1024]{1,0:T(8,128)S(1)}, f32[8,1024]{1,0:T(8,128)}, u32[]{:S(2)}) copy-start(f32[8,1024]{1,0:T(8,128)} %get-tuple-element.454) | copy-start | bytes 98308
  353.9 80.5 %copy-start.22 = (f32[8,1024]{1,0:T(8,128)S(1)}, f32[8,1024]{1,0:T(8,128)}, u32[]{:S(2)}) copy-start(f32[8,1024]{1,0:T(8,128)} %get-tuple-element.451) | copy-start | bytes 98308
  353.9 80.5 %copy-start.26 = (f32[8,1024]{1,0:T(8,128)S(1)}, f32[8,1024]{1,0:T(8,128)}, u32[]{:S(2)}) copy-start(f32[8,1024]{1,0:T(8,128)} %get-tuple-element.450) | copy-start | bytes 98308
  353.9 255.6 %reduce-scatter.10.cloned.1.call-start = ((), (), s32[]{:S(2)}) async-start(), calls=%async_computation.10 | async-start | bytes 5242880 | tf_op jit(solution)/shard_map/reduce_scatter | solution.py:161
  435.8 26.6 %collective-permute-start = (bf16[1,8,64,1024]{3,2,1,0:T(8,128)(2,1)}, bf16[1,8,64,1024]{3,2,1,0:T(8,128)(2,1)S(1)}, u32[]{:S(2)}, u32[]{:S(2)}) collective-permute-start(bf16[1,8,64,1024]{3,2,1,0:T(8,128)(2,1)} %add_convert_fusion), channel_id=1, source_target_pairs={{0,1},{1,2},{2,3},{3,0},{4,5},{5,6},{6,7},{7,4},{8,9},{9,10},{10,1... | collective-permute-start | bytes 3145736 | tf_op jit(solution)/shard_map/ppermute | solution.py:20
  462.4 27.9 %collective-permute-start.1 = (bf16[1,8,64,1024]{3,2,1,0:T(8,128)(2,1)S(1)}, bf16[1,8,64,1024]{3,2,1,0:T(8,128)(2,1)}, u32[]{:S(2)}, u32[]{:S(2)}) collective-permute-start(bf16[1,8,64,1024]{3,2,1,0:T(8,128)(2,1)S(1)} %collective-permute-done), channel_id=1, source_target_pairs={{0,1},{1,2},{2,3},{3,0},{4,5},{5,6},{6,7},{7,4},{8,9},{9,10},{10,1... | collective-permute-start | bytes 3145736 | tf_op jit(solution)/shard_map/ppermute | solution.py:20
  462.4 46.7 %collective-permute-start.2 = (bf16[1,8,64,1024]{3,2,1,0:T(8,128)(2,1)}, bf16[1,8,64,1024]{3,2,1,0:T(8,128)(2,1)}, u32[]{:S(2)}, u32[]{:S(2)}) collective-permute-start(bf16[1,8,64,1024]{3,2,1,0:T(8,128)(2,1)} %add_convert_fusion), channel_id=1, source_target_pairs={{0,3},{1,0},{2,1},{3,2},{4,7},{5,4},{6,5},{7,6},{8,11},{9,8},{10,9... | collective-permute-start | bytes 3145736 | tf_op jit(solution)/shard_map/ppermute | solution.py:23
  466.2 228.6 %copy-start.47 = (f32[1024]{0:T(1024)}, f32[1024]{0:T(1024)S(1)}, u32[]{:S(2)}) copy-start(f32[1024]{0:T(1024)S(1)} %convert_element_type.268) | copy-start | bytes 12292
  531.8 77.7 %copy-start.28 = (f32[8,1024]{1,0:T(8,128)S(1)}, f32[8,1024]{1,0:T(8,128)}, u32[]{:S(2)}) copy-start(f32[8,1024]{1,0:T(8,128)} %get-tuple-element.449) | copy-start | bytes 98308
  531.8 163.0 %all-gather.11.cloned.1.call-start = ((), (), s32[]{:S(2)}) async-start(), calls=%async_computation.11 | async-start | bytes 5242880 | tf_op jit(solution)/shard_map/all_gather | solution.py:175
  613.4 179.0 %reduce-scatter.12.cloned.1.call-start = ((), (), s32[]{:S(2)}) async-start(), calls=%async_computation.12 | async-start | bytes 5242880 | tf_op jit(solution)/shard_map/reduce_scatter | solution.py:184
  716.9 78.4 %copy-start.18 = (bf16[64,1,8,1024]{3,0,2,1:T(8,128)(2,1)S(1)}, bf16[64,1,8,1024]{3,0,2,1:T(8,128)(2,1)}, u32[]{:S(2)}) copy-start(bf16[64,1,8,1024]{3,0,2,1:T(8,128)(2,1)} %reduce-scatter.8.cloned.1.call-done) | copy-start | bytes 3145732
  716.9 166.9 %all-gather.13.cloned.1.call-start = ((), (), s32[]{:S(2)}) async-start(), calls=%async_computation.13 | async-start | bytes 5242880 | tf_op jit(solution)/shard_map/all_gather | solution.py:199
  799.8 84.0 %copy-start.27 = (bf16[256,1024]{1,0:T(8,128)(2,1)S(1)}, bf16[256,1024]{1,0:T(8,128)(2,1)}, u32[]{:S(2)}) copy-start(bf16[256,1024]{1,0:T(8,128)(2,1)} %param.21) | copy-start | bytes 1572868
  802.5 545.8 %reduce-scatter.14.cloned.1.call-start = ((), (), s32[]{:S(2)}) async-start(), calls=%async_computation.14 | async-start | bytes 3145728 | tf_op jit(solution)/shard_map/reduce_scatter | solution.py:253
  1336.4 22.1 %reduce-scatter.16.cloned.1.call-start = ((), (), s32[]{:S(2)}) async-start(), calls=%async_computation.15 | async-start | bytes 3145728 | tf_op jit(solution)/shard_map/reduce_scatter | solution.py:259
  1345.4 99.0 %reduce-scatter.18.cloned.1.call-start = ((), (), s32[]{:S(2)}) async-start(), calls=%async_computation.16 | async-start | bytes 5242880 | tf_op jit(solution)/shard_map/reduce_scatter | solution.py:279
  1366.1 102.9 %reduce-scatter.20.cloned.1.call-start = ((), (), s32[]{:S(2)}) async-start(), calls=%async_computation.17 | async-start | bytes 122880 | tf_op jit(solution)/shard_map/reduce_scatter | solution.py:304
  1449.0 162.1 %all-reduce.7.cloned.1.call-start = ((), (), s32[]{:S(2)}) async-start(), calls=%async_computation.19 | async-start | bytes 18874368 | tf_op jit(solution)/shard_map/psum | solution.py:329
  (59 other events, 882.4 us)
Sparse Core Ops, SparseCore 0:
  21.4 83.4 all-gather.6
  114.6 9.0 all-gather.8
  125.8 11.7 all-gather.14
  354.0 76.7 reduce-scatter.7
  532.0 77.4 reduce-scatter.9
  613.5 81.2 all-gather.10
  717.1 75.2 reduce-scatter.11
  802.6 81.2 all-gather.12
  1336.6 8.2 reduce-scatter.13
  1347.5 11.0 reduce-scatter.15
  1366.2 78.0 reduce-scatter.17
  1449.1 19.8 reduce-scatter.19
  1474.5 136.5 all-reduce.6
